TPU v7x, 256 devices: a whole 4x4x8 slice. The times are simulated.
256 devices in a mesh: dp: 32 (over x, y, core), seq: 8 (over z).
Axes of the slice: x: 4, y: 4, z: 8, core: 2. Of those that a mesh axis runs over, the one named last changes fastest.
Arguments:
- tokens: bfloat16 [32, 2048, 5120], P('dp', 'seq'), may hold values from -6 to 6
- queries: bfloat16 [32, 2048, 2560], P('dp', 'seq'), may hold values from -400 to 400
- cotangent: bfloat16 [32, 2048, 2560], P('dp', 'seq'), may hold values from -6 to 6
- kv_weight: bfloat16 [5120, 1024], P('dp'), may hold values from -0.078125 to 0.078125
- active: int32 [32, 8], P('dp'), may hold values from 0 to 15, as said below
Outputs:
- query_grads: bfloat16 [32, 2048, 2560], P('dp', 'seq')
- token_grads: bfloat16 [32, 2048, 5120], P('dp', 'seq')
- weight_grad: float32 [5120, 1024], P('dp', 'seq')
Inputs may be any that keep to these rules, and one draw needn't show every extreme that they name: active[p] lists 8 different blocks of sequence p in increasing order; blocks 0 and 15 are always among them.
All inputs are finite; a program needn't handle non-finite values.
Results may differ from a plain program's by a relative error of at most 0.019.
The roundings to bfloat16 on the way count: a program that leaves them out, or rounds other values in their place, can miss the bound.
Values may be sent and summed in bfloat16 or wider, within the bound.
A program may use at most 128 MiB of HBM per device.

v0:
```python
import math

import jax
import jax.numpy as jnp
from jax import lax
from jax.sharding import PartitionSpec as P

HEAD_SIZE = 128
BLK = 128


def body(tokens, queries, cotangent, kv_weight, active):
    seq_count = lax.axis_size("seq")
    seq_rank = lax.axis_index("seq")
    tok_dev = tokens.shape[1]
    qwidth = queries.shape[2]
    kvwidth = kv_weight.shape[1]
    row_count = BLK // seq_count
    blocks_dev = tok_dev // BLK
    block_total = blocks_dev * seq_count
    act_total = active.shape[1]
    kv_heads = kvwidth // (2 * HEAD_SIZE)
    head_group = qwidth // (HEAD_SIZE * kv_heads)
    scale = 1.0 / math.sqrt(HEAD_SIZE)
    weight_full = lax.all_gather(kv_weight, "dp", axis=0, tiled=True)
    x_local = tokens[0]
    keyval = jnp.dot(x_local, weight_full, preferred_element_type=jnp.float32).astype(jnp.bfloat16)

    def spread(values_in):
        return values_in.reshape(blocks_dev, seq_count, row_count, values_in.shape[-1])

    q_in, g_in, kv_in = (
        lax.all_to_all(spread(queries[0]), "seq", split_axis=1, concat_axis=0, tiled=True),
        lax.all_to_all(spread(cotangent[0]), "seq", split_axis=1, concat_axis=0, tiled=True),
        lax.all_to_all(spread(keyval), "seq", split_axis=1, concat_axis=0, tiled=True),
    )
    block_ids = active[0]
    active_query = q_in.reshape(block_total, row_count, qwidth)[block_ids]
    active_gradient = g_in.reshape(block_total, row_count, qwidth)[block_ids]
    kv_act = kv_in.reshape(block_total, row_count, kvwidth)[block_ids]
    kv_all = lax.all_gather(kv_act, "seq", axis=1, tiled=True)
    query_rows = act_total * row_count
    key_count = act_total * BLK
    kv_flat = kv_all.reshape(key_count, kvwidth)
    key_matrix = kv_flat[:, : kv_heads * HEAD_SIZE].reshape(key_count, kv_heads, HEAD_SIZE)
    value_matrix = kv_flat[:, kv_heads * HEAD_SIZE :].reshape(key_count, kv_heads, HEAD_SIZE)
    q_heads = active_query.reshape(query_rows, kv_heads, head_group, HEAD_SIZE)
    g_heads = active_gradient.reshape(query_rows, kv_heads, head_group, HEAD_SIZE)
    scores = (
        jnp.einsum("mkgd,nkd->kgmn", q_heads, key_matrix, preferred_element_type=jnp.float32)
        * scale
    )
    query_pos = (
        jnp.arange(act_total, dtype=jnp.int32)[:, None] * BLK
        + seq_rank * row_count
        + jnp.arange(row_count, dtype=jnp.int32)[None, :]
    ).reshape(query_rows)
    causal = jnp.arange(key_count, dtype=jnp.int32)[None, :] <= query_pos[:, None]
    scores = jnp.where(causal, scores, -1e30)
    row_max = jnp.max(scores, axis=-1, keepdims=True)
    exponent = jnp.exp(scores - row_max)
    probs = exponent / jnp.sum(exponent, axis=-1, keepdims=True)
    probs_low = probs.astype(jnp.bfloat16)
    attended = jnp.einsum(
        "kgmn,nkd->mkgd", probs_low, value_matrix, preferred_element_type=jnp.float32
    )
    row_delta = jnp.einsum("mkgd,mkgd->kgm", g_heads.astype(jnp.float32), attended)
    dprobs = jnp.einsum("mkgd,nkd->kgmn", g_heads, value_matrix, preferred_element_type=jnp.float32)
    dscores = (probs * (dprobs - row_delta[..., None]) * scale).astype(jnp.bfloat16)
    query_grad = jnp.einsum(
        "kgmn,nkd->mkgd", dscores, key_matrix, preferred_element_type=jnp.float32
    ).astype(jnp.bfloat16)
    query_grad = query_grad.reshape(act_total, row_count, qwidth)
    key_gradient = jnp.einsum(
        "kgmn,mkgd->nkd", dscores, q_heads, preferred_element_type=jnp.float32
    )
    value_gradient = jnp.einsum(
        "kgmn,mkgd->nkd", probs_low, g_heads, preferred_element_type=jnp.float32
    )
    kv_terms = jnp.concatenate(
        [
            key_gradient.reshape(key_count, kv_heads * HEAD_SIZE),
            value_gradient.reshape(key_count, kv_heads * HEAD_SIZE),
        ],
        axis=1,
    )
    kv_terms = kv_terms.reshape(act_total, BLK, kvwidth)
    kv_mine = lax.psum_scatter(kv_terms, "seq", scatter_dimension=1, tiled=True).astype(
        jnp.bfloat16
    )

    def padded(values_in):
        width_here = values_in.shape[-1]
        placed = (
            jnp.zeros((block_total, row_count, width_here), jnp.bfloat16)
            .at[block_ids]
            .set(values_in)
        )
        return placed.reshape(seq_count, blocks_dev, 1, row_count, width_here)

    query_back, kv_back = (
        lax.all_to_all(padded(query_grad), "seq", split_axis=0, concat_axis=2, tiled=True),
        lax.all_to_all(padded(kv_mine), "seq", split_axis=0, concat_axis=2, tiled=True),
    )
    query_back = query_back.reshape(tok_dev, qwidth)
    kv_back = kv_back.reshape(tok_dev, kvwidth)
    token_grad = lax.dot_general(
        kv_back, weight_full, (((1,), (1,)), ((), ())), preferred_element_type=jnp.float32
    ).astype(jnp.bfloat16)
    partial_value = lax.dot_general(
        x_local, kv_back, (((0,), (0,)), ((), ())), preferred_element_type=jnp.float32
    )
    part_sum = lax.psum_scatter(
        partial_value.astype(jnp.bfloat16), "dp", scatter_dimension=0, tiled=True
    ).astype(jnp.float32)
    weight_part = lax.psum_scatter(part_sum, "seq", scatter_dimension=1, tiled=True)
    return (query_back[None], token_grad[None], weight_part)


def solution(mesh):
    in_specs = (
        P("dp", "seq", None),
        P("dp", "seq", None),
        P("dp", "seq", None),
        P("dp", None),
        P("dp", None),
    )
    out_specs = (P("dp", "seq", None), P("dp", "seq", None), P("dp", "seq"))
    return jax.shard_map(body, mesh=mesh, in_specs=in_specs, out_specs=out_specs, check_vma=False)
```

profile of v0, /device:TPU:2, one launch (start us, length us, event | category | flops | bytes accessed | tf_op | source)
XLA Modules:
  0.0 497.3 jit_solution(6844400234804034998)
XLA Ops:
  7.9 68.3 %all-gather.4.cloned.1.call-done = bf16[5120,1024]{1,0:T(8,128)(2,1)} async-done(((bf16[160,1024]{1,0:T(8,128)(2,1)}), bf16[5120,1024]{1,0:T(8,128)(2,1)}) %all-gather.4.cloned.1.call-update) | async-done | bytes 10485776 | tf_op jit(solution)/shard_map/all_gather | solution.py:25
  76.2 6.8 %fusion.14 = bf16[256,1024]{1,0:T(8,128)(2,1)S(1)} fusion(bf16[5120,1024]{1,0:T(8,128)(2,1)} %all-gather.4.cloned.1.call-done, bf16[1,256,5120]{2,1,0:T(8,128)(2,1)S(1)} %copy-done), kind=kOutput, calls=%fused_computation.28 | convolution fusion | flops 2684616704 | bytes 13631488 | tf_op jit(solution)/shard_map/dot_general | solution.py:27
  83.9 7.0 %all-to-all-start = ((bf16[2,8,16,1024]{3,2,0,1:T(8,128)(2,1)}), bf16[2,8,16,1024]{3,2,0,1:T(8,128)(2,1)S(1)}, u32[]{:S(2)}, u32[]{:S(2)}) async-start(bf16[2,8,16,1024]{3,2,0,1:T(8,128)(2,1)} %copy.53), calls=%async_computation | async-start | bytes 1048576 | tf_op jit(solution)/shard_map/all_to_all | solution.py:35
  90.9 2.5 copy.59
  93.4 15.5 %all-to-all-done = bf16[2,8,16,1024]{3,2,0,1:T(8,128)(2,1)S(1)} async-done(((bf16[2,8,16,1024]{3,2,0,1:T(8,128)(2,1)}), bf16[2,8,16,1024]{3,2,0,1:T(8,128)(2,1)S(1)}, u32[]{:S(2)}, u32[]{:S(2)}) %all-to-all-start) | async-done | bytes 524320 | tf_op jit(solution)/shard_map/all_to_all | solution.py:35
  108.8 4.3 all-to-all-start.2
  113.2 1.3 gather_fusion
  114.5 2.5 copy.55
  117.0 39.4 %all-to-all-done.2 = bf16[2,8,16,2560]{3,2,0,1:T(8,128)(2,1)} async-done(((bf16[2,8,16,2560]{3,2,0,1:T(8,128)(2,1)}), bf16[2,8,16,2560]{3,2,0,1:T(8,128)(2,1)}, u32[]{:S(2)}, u32[]{:S(2)}) %all-to-all-start.2) | async-done | bytes 1310752 | tf_op jit(solution)/shard_map/all_to_all | solution.py:34
  156.4 4.3 all-to-all-start.1
  161.1 1.9 gather_fusion.2
  163.1 1.7 reshape.117
  164.8 2.4 copy.69
  167.2 2.8 bitcast_convert_fusion
  170.0 2.7 copy.85
  172.7 23.0 %all-to-all-done.1 = bf16[2,8,16,2560]{3,2,0,1:T(8,128)(2,1)} async-done(((bf16[2,8,16,2560]{3,2,0,1:T(8,128)(2,1)}), bf16[2,8,16,2560]{3,2,0,1:T(8,128)(2,1)}, u32[]{:S(2)}, u32[]{:S(2)}) %all-to-all-start.1) | async-done | bytes 1310752 | tf_op jit(solution)/shard_map/all_to_all | solution.py:33
  195.6 1.9 gather_fusion.1
  197.5 1.7 reshape.114
  199.3 1.7 copy.67
  201.0 3.1 fusion.24
  204.1 2.3 copy.98
  206.4 2.3 copy.99
  208.7 8.6 %fusion.25 = (f32[4,5,128]{2,1,0:T(8,128)S(1)}, f32[4,5,128,1024]{2,3,1,0:T(8,128)}) fusion(pred[128,1024]{0,1:T(8,128)(4,1)S(1)} %iota_compare_fusion, bf16[1024,4,128,1]{0,2,3,1:T(8,128)(2,1)} %bitcast.139, bf16[128,4,5,128]{0,3,2,1:T(8,128)(2,1)S(1)} %copy.67), kind=kOutput, calls=%fused_computation.42 | convolution fusion | flops 681575424 | bytes 12331008 | tf_op jit(solution)/shard_map/sub | solution.py:61
  217.3 5.5 %fusion.9 = bf16[4,5,128,1024]{2,3,1,0:T(8,128)(2,1)S(1)} fusion(f32[4,5,128,1024]{2,3,1,0:T(8,128)} %get-tuple-element.18, f32[4,5,128]{2,1,0:T(8,128)S(1)} %get-tuple-element.17), kind=kLoop, calls=%fused_computation.20 | loop fusion | flops 5242880 | bytes 15738880 | tf_op jit(solution)/shard_map/convert_element_type | solution.py:63
  222.8 1.8 fusion.27
  226.8 3.8 fusion.3
  230.6 1.8 copy.101
  232.3 2.9 copy.72
  235.3 4.2 fusion.26
  239.5 1.8 copy.100
  241.3 3.0 copy.71
  244.3 4.8 pad_maximum_fusion
  249.2 52.9 %reduce-scatter.6.cloned.1.call-done = f32[8,16,1024]{2,1,0:T(8,128)} async-done(((f32[8,128,1024]{2,1,0:T(8,128)}), f32[8,16,1024]{2,1,0:T(8,128)}) %reduce-scatter.6.cloned.1.call-update) | async-done | bytes 524304 | tf_op jit(solution)/shard_map/reduce_scatter | solution.py:88
  304.0 21.6 %all_to_all.75 = bf16[8,2,1,16,1024]{4,3,1,2,0:T(8,128)(2,1)S(1)} all-to-all(bf16[8,2,1,16,1024]{4,3,1,2,0:T(8,128)(2,1)S(1)} %bitcast.143), channel_id=1, replica_groups=mesh['dp'=32,'seq'=8] {'seq'}, dimensions={0} | all-to-all | bytes 1048576 | tf_op jit(solution)/shard_map/all_to_all | solution.py:103
  326.4 5.5 %convert_bitcast_fusion = bf16[5120,1024]{0,1:T(8,128)(2,1)} fusion(bf16[256,1024]{1,0:T(8,128)(2,1)S(1)} %bitcast.145, bf16[1,256,5120]{2,1,0:T(8,128)(2,1)S(1)} %copy-done), kind=kOutput, calls=%fused_computation.11 | convolution fusion | flops 2689597440 | bytes 13631488 | tf_op jit(solution)/shard_map/dot_general | solution.py:110
  331.9 14.4 %copy.96 = bf16[5120,1024]{1,0:T(8,128)(2,1)} copy(bf16[5120,1024]{0,1:T(8,128)(2,1)} %convert_bitcast_fusion) | data formatting | bytes 20971520
  346.3 3.8 fusion.18
  350.1 1.7 copy.64
  351.8 1.9 reshape.150
  353.6 1.2 broadcast_in_dim.14
  354.8 2.6 scatter_fusion
  357.5 4.3 all-to-all-start.3
  361.8 86.2 %reduce-scatter.10.cloned.1.call-done = bf16[160,1024]{1,0:T(8,128)(2,1)} async-done(((bf16[5120,1024]{1,0:T(8,128)(2,1)}), bf16[160,1024]{1,0:T(8,128)(2,1)}) %reduce-scatter.10.cloned.1.call-update) | async-done | bytes 327696
  448.0 1.2 copy.97
  450.3 2.5 copy.66
  452.7 8.6 %fusion.5 = bf16[1,256,5120]{2,1,0:T(8,128)(2,1)} fusion(bf16[256,1024]{1,0:T(8,128)(2,1)} %bitcast.146, bf16[5120,1024]{1,0:T(8,128)(2,1)} %all-gather.4.cloned.1.call-done), kind=kOutput, calls=%fused_computation.15 | convolution fusion | flops 2685665280 | bytes 13631488 | tf_op jit(solution)/shard_map/dot_general | solution.py:107
  461.3 27.8 %reduce-scatter.8.cloned.1.call-done = f32[160,128]{0,1:T(8,128)} async-done(((f32[160,1024]{0,1:T(8,128)}), f32[160,128]{0,1:T(8,128)}) %reduce-scatter.8.cloned.1.call-update) | async-done | bytes 81936 | tf_op jit(solution)/shard_map/reduce_scatter | solution.py:116
  489.1 1.6 copy.75
  (39 shorter events, 8.2 us)
Async XLA Ops:
  7.2 69.0 %copy-start = (bf16[1,256,5120]{2,1,0:T(8,128)(2,1)S(1)}, bf16[1,256,5120]{2,1,0:T(8,128)(2,1)}, u32[]{:S(2)}) copy-start(bf16[1,256,5120]{2,1,0:T(8,128)(2,1)} %param.5) | copy-start | bytes 7864324
  7.2 69.0 %all-gather.4.cloned.1.call-start = ((), (), s32[]{:S(2)}) async-start(), calls=%async_computation.8 | async-start | bytes 10813440 | tf_op jit(solution)/shard_map/all_gather | solution.py:25
  83.0 30.1 %copy-start.6 = (s32[1,8]{1,0:T(1,128)S(1)}, s32[1,8]{1,0:T(1,128)}, u32[]{:S(2)}) copy-start(s32[1,8]{1,0:T(1,128)} %param.9) | copy-start | bytes 100
  83.9 24.9 %all-to-all-start = ((bf16[2,8,16,1024]{3,2,0,1:T(8,128)(2,1)}), bf16[2,8,16,1024]{3,2,0,1:T(8,128)(2,1)S(1)}, u32[]{:S(2)}, u32[]{:S(2)}) async-start(bf16[2,8,16,1024]{3,2,0,1:T(8,128)(2,1)} %copy.53), calls=%async_computation | async-start | bytes 1048576 | tf_op jit(solution)/shard_map/all_to_all | solution.py:35
  108.8 47.5 %all-to-all-start.2 = ((bf16[2,8,16,2560]{3,2,0,1:T(8,128)(2,1)}), bf16[2,8,16,2560]{3,2,0,1:T(8,128)(2,1)}, u32[]{:S(2)}, u32[]{:S(2)}) async-start(bf16[2,8,16,2560]{3,2,0,1:T(8,128)(2,1)} %copy.59), calls=%async_computation.2 | async-start | bytes 2621440 | tf_op jit(solution)/shard_map/all_to_all | solution.py:34
  113.1 87.9 %all-gather.6.cloned.1.call-start = ((), (), s32[]{:S(2)}) async-start(), calls=%async_computation.11 | async-start | bytes 2359296 | tf_op jit(solution)/shard_map/all_gather | solution.py:41
  156.4 39.3 %all-to-all-start.1 = ((bf16[2,8,16,2560]{3,2,0,1:T(8,128)(2,1)}), bf16[2,8,16,2560]{3,2,0,1:T(8,128)(2,1)}, u32[]{:S(2)}, u32[]{:S(2)}) async-start(bf16[2,8,16,2560]{3,2,0,1:T(8,128)(2,1)} %copy.55), calls=%async_computation.1 | async-start | bytes 2621440 | tf_op jit(solution)/shard_map/all_to_all | solution.py:33
  160.6 141.4 %reduce-scatter.6.cloned.1.call-start = ((), (), s32[]{:S(2)}) async-start(), calls=%async_computation.9 | async-start | bytes 4718592 | tf_op jit(solution)/shard_map/reduce_scatter | solution.py:88
  217.3 5.5 %copy-start.4 = (bf16[128,4,5,128]{0,3,2,1:T(8,128)(2,1)S(1)}, bf16[128,4,5,128]{0,3,2,1:T(8,128)(2,1)}, u32[]{:S(2)}) copy-start(bf16[128,4,5,128]{0,3,2,1:T(8,128)(2,1)} %copy.69) | copy-start | bytes 1966084
  217.3 7.3 %copy-start.2 = (f32[4,5,128,128]{2,3,1,0:T(8,128)S(1)}, f32[4,5,128,128]{2,3,1,0:T(8,128)}, u32[]{:S(2)}) copy-start(f32[4,5,128,128]{2,3,1,0:T(8,128)} %copy.85) | copy-start | bytes 3932164
  217.3 7.3 %copy-start.3 = (bf16[1024,512]{0,1:T(8,128)(2,1)S(1)}, bf16[1024,512]{0,1:T(8,128)(2,1)}, u32[]{:S(2)}) copy-start(bf16[1024,512]{0,1:T(8,128)(2,1)} %copy.99) | copy-start | bytes 3145732
  222.8 4.0 copy-start.1
  249.1 198.8 %reduce-scatter.10.cloned.1.call-start = ((), (), s32[]{:S(2)}) async-start(), calls=%async_computation.12 | async-start | bytes 10813440
  325.6 0.8 copy-start.5
  357.5 92.8 %all-to-all-start.3 = ((bf16[8,2,1,16,2560]{4,3,1,2,0:T(8,128)(2,1)}), bf16[8,2,1,16,2560]{4,3,1,2,0:T(8,128)(2,1)}, u32[]{:S(2)}, u32[]{:S(2)}) async-start(bf16[8,2,1,16,2560]{4,3,1,2,0:T(8,128)(2,1)} %bitcast.138), calls=%async_computation.3 | async-start | bytes 2621440 | tf_op jit(solution)/shard_map/all_to_all | solution.py:102
  361.8 127.3 %reduce-scatter.8.cloned.1.call-start = ((), (), s32[]{:S(2)}) async-start(), calls=%async_computation.10 | async-start | bytes 1179648 | tf_op jit(solution)/shard_map/reduce_scatter | solution.py:116
Sparse Core Ops, SparseCore 0:
  10.5 65.6 all-gather.3
  115.7 62.6 all-gather.5
  249.3 52.7 reduce-scatter.5
  346.4 101.5 reduce-scatter.9
  450.4 38.6 reduce-scatter.7
where the time goes:
time: 499 us; the launch traced here: 497 us
  waiting for transfers between devices  314 us (63%)
  local copies, waits for them, and re-layouts  68.2 us (14%)
  matrix products  44.1 us (9%)
  blocking collectives  21.6 us (4%)
  starting transfers between devices  20.2 us (4%)
  other arithmetic  15.5 us (3%)
  between operations  14 us (3%)
    unnamed x6, waiting for transfers between devices  86.9 us
    all_gather x1, waiting for transfers between devices, body(): weight_full = lax.all_gather(kv_weight, 'dp', axis=0, tiled=True)  68.3 us
    reduce_scatter x1, waiting for transfers between devices, body(): lax.psum_scatter(kv_terms, 'seq', scatter_dimension=1, tiled=True)  52.9 us
    all_to_all x1, waiting for transfers between devices, body(): lax.all_to_all(spread(cotangent[0]), 'seq', split_axis=1, concat_axis=0,...  39.4 us
    unnamed x22, local copies, waits for them, and re-layouts  30 us
    reduce_scatter x1, waiting for transfers between devices, body(): lax.psum_scatter(part_sum, 'seq', scatter_dimension=1, tiled=True)  27.8 us
    all_to_all x1, waiting for transfers between devices, body(): lax.all_to_all(spread(queries[0]), 'seq', split_axis=1, concat_axis=0, ti...  23 us
    all_to_all x1, blocking collectives, body(): lax.all_to_all(padded(kv_mine), 'seq', split_axis=0, concat_axis=2, tiled...  21.6 us
  transfers between devices with their start and end apart: 9, of which 7 were waited for; matrix products, arithmetic and copies ran while one was open for 10% of the time, Pallas kernels for 0%

commit v1 on v0

v1 whole, which is shorter than its diff:
```python
import math

import jax
import jax.numpy as jnp
from jax import lax
from jax.experimental import pallas as pl
from jax.experimental.pallas import tpu as pltpu
from jax.sharding import PartitionSpec as P

HEAD = 128
BLK = 128
NBLK = 16
NACT = 8
KVH = 4
GRP = 5
HALF = 64
ROWS = GRP * HALF
BF = jnp.bfloat16
F32 = jnp.float32
MESH = pl.DeviceIdType.MESH
VM = pl.BlockSpec(memory_space=pltpu.VMEM)
NT = (((1,), (1,)), ((), ()))


def attention_kernel(act, q_ref, g_ref, kv_ref, qg_ref, dkv_ref, kc, vc, sc, dp, pb, ds, dkt, dvt):
    scale = 1.0 / math.sqrt(HEAD)
    half = act[NACT]
    for j in range(NACT):
        block = kv_ref[act[j]]
        kc[j * BLK : (j + 1) * BLK, :] = block[:, :HEAD]
        vc[j * BLK : (j + 1) * BLK, :] = block[:, HEAD:]
    qg_ref[...] = jnp.zeros_like(qg_ref)
    dkv_ref[...] = jnp.zeros_like(dkv_ref)
    step = 32
    for a in reversed(range(NACT)):
        n = (a + 1) * BLK
        b = act[a]
        q5 = jnp.concatenate([q_ref[b, :, i * HEAD : (i + 1) * HEAD] for i in range(GRP)], axis=0)
        g5 = jnp.concatenate([g_ref[b, :, i * HEAD : (i + 1) * HEAD] for i in range(GRP)], axis=0)
        sc[:, :n] = lax.dot_general(q5, kc[:n, :], NT, preferred_element_type=F32)
        dp[:, :n] = lax.dot_general(g5, vc[:n, :], NT, preferred_element_type=F32)

        def softmax(i, carry):
            rows = pl.ds(pl.multiple_of(i * step, step), step)
            s = sc[rows, :n] * scale
            pos = half * HALF + lax.rem(i, HALF // step) * step + lax.broadcasted_iota(jnp.int32, (step, BLK), 0)
            col = lax.broadcasted_iota(jnp.int32, (step, BLK), 1)
            last = jnp.where(col <= pos, s[:, n - BLK :], -1e30)
            s = last if a == 0 else jnp.concatenate([s[:, : n - BLK], last], axis=1)
            e = jnp.exp(s - jnp.max(s, axis=-1, keepdims=True))
            p = e / jnp.sum(e, axis=-1, keepdims=True)
            low = p.astype(BF)
            d = dp[rows, :n]
            delta = jnp.sum(low.astype(F32) * d, axis=-1, keepdims=True)
            pb[rows, :n] = low
            ds[rows, :n] = (p * (d - delta) * scale).astype(BF)
            return carry

        lax.fori_loop(0, ROWS // step, softmax, 0)
        dq = jnp.dot(ds[:, :n], kc[:n, :], preferred_element_type=F32).astype(BF)
        for i in range(GRP):
            qg_ref[b, :, i * HEAD : (i + 1) * HEAD] = dq[i * HALF : (i + 1) * HALF, :]
        dk = jnp.dot(q5.T, ds[:, :n], preferred_element_type=F32)
        dv = jnp.dot(g5.T, pb[:, :n], preferred_element_type=F32)
        if a == NACT - 1:
            dkt[...] = dk
            dvt[...] = dv
        else:
            dkt[:, :n] += dk
            dvt[:, :n] += dv
    for j in range(NACT):
        b = act[j]
        dkv_ref[b, :, :HEAD] = dkt[:, j * BLK : (j + 1) * BLK].T.astype(BF)
        dkv_ref[b, :, HEAD:] = dvt[:, j * BLK : (j + 1) * BLK].T.astype(BF)


def attention(act, q, g, kv):
    n = NACT * BLK
    return pl.pallas_call(
        attention_kernel,
        out_shape=(jax.ShapeDtypeStruct(q.shape, BF), jax.ShapeDtypeStruct(kv.shape, BF)),
        in_specs=[pl.BlockSpec(memory_space=pltpu.SMEM), VM, VM, VM],
        out_specs=(VM, VM),
        scratch_shapes=[
            pltpu.VMEM((n, HEAD), BF),
            pltpu.VMEM((n, HEAD), BF),
            pltpu.VMEM((ROWS, n), F32),
            pltpu.VMEM((ROWS, n), F32),
            pltpu.VMEM((ROWS, n), BF),
            pltpu.VMEM((ROWS, n), BF),
            pltpu.VMEM((HEAD, n), F32),
            pltpu.VMEM((HEAD, n), F32),
        ],
        name="attention",
    )(act, q, g, kv)


def grad_kernel(x_ref, dk_ref, out_ref, kvb_ref, kv2, total, s1, r1, s2, r2, s3, r3, mine, ssem, rsem):
    me = lax.axis_index("dp")
    z = lax.axis_index("seq")
    c = lax.rem(me, 2)
    cy = lax.rem(me // 2, 4)
    cx = me // 8
    f = cx + (cy - cx) * c
    s = cy + (cx - cy) * c

    def device(ff, ss):
        return ff * (8 - 6 * c) + ss * (2 + 6 * c) + c

    partner = me + 1 - 2 * c
    f_right, f_left, f_far = lax.rem(f + 1, 4), lax.rem(f + 3, 4), lax.rem(f + 2, 4)
    s_right, s_left, s_far = lax.rem(s + 1, 4), lax.rem(s + 3, 4), lax.rem(s + 2, 4)
    right1, left1 = device(f_right, s), device(f_left, s)
    right2, left2 = device(f, s_right), device(f, s_left)

    barrier = pltpu.get_barrier_semaphore()
    for peer in (partner, right1, left1, right2, left2):
        pl.semaphore_signal(barrier, inc=1, device_id=(peer, z), device_id_type=MESH)
    for k in range(1, 8):
        pl.semaphore_signal(barrier, inc=1, device_id=(me, lax.rem(z + k, 8)), device_id_type=MESH)
    for h in range(KVH):
        for part in range(2):
            lanes = slice(part * HEAD, (part + 1) * HEAD)
            both = dk_ref[2 * h, :, lanes].astype(F32) + dk_ref[2 * h + 1, :, lanes].astype(F32)
            kv2[0:256, (part * KVH + h) * HEAD : (part * KVH + h + 1) * HEAD] = both.astype(BF)
    pl.semaphore_wait(barrier, 12)

    def send(index, src, dst, dev, seq):
        copy = pltpu.make_async_remote_copy(
            src_ref=src,
            dst_ref=dst,
            send_sem=ssem.at[index],
            recv_sem=rsem.at[index],
            device_id=(dev, seq),
            device_id_type=MESH,
        )
        copy.start()
        return copy

    swap = send(0, kv2.at[0:256], kv2.at[256:512], partner, z)
    kvb_ref[...] = kv2[0:256, :]
    swap.wait()

    def product(ff, part):
        return jnp.dot(x_ref[ff, part * 320 : (part + 1) * 320, :], kv2[...], preferred_element_type=F32)

    s1[0] = product(f_far, 0).astype(BF)
    far_r = send(1, s1.at[0], r1.at[0], right1, z)
    s1[1] = product(f_far, 1).astype(BF)
    far_l = send(2, s1.at[1], r1.at[1], left1, z)
    s1[2] = product(f_right, 1).astype(BF)
    own_r = send(3, s1.at[2], r1.at[2], right1, z)
    s1[3] = product(f_left, 0).astype(BF)
    own_l = send(4, s1.at[3], r1.at[3], left1, z)
    total[0:2] = product(f_right, 0).reshape(2, 160, 1024)
    far_r.wait_recv()
    s1[4] = (total[0:2].reshape(320, 1024) + r1[0].astype(F32)).astype(BF)
    sum_r = send(5, s1.at[4], r1.at[4], right1, z)
    total[2:4] = product(f_left, 1).reshape(2, 160, 1024)
    far_l.wait_recv()
    s1[5] = (total[2:4].reshape(320, 1024) + r1[1].astype(F32)).astype(BF)
    sum_l = send(6, s1.at[5], r1.at[5], left1, z)
    total[0:2] = product(f, 0).reshape(2, 160, 1024)
    total[2:4] = product(f, 1).reshape(2, 160, 1024)
    own_r.wait_recv()
    own_l.wait_recv()
    total[0:2] += r1[3].astype(F32).reshape(2, 160, 1024)
    total[2:4] += r1[2].astype(F32).reshape(2, 160, 1024)
    sum_r.wait_recv()
    total[0:2] += r1[4].astype(F32).reshape(2, 160, 1024)
    sum_l.wait_recv()
    total[2:4] += r1[5].astype(F32).reshape(2, 160, 1024)

    s2[0] = total[s_far, 0:80, :].astype(BF)
    far_r2 = send(7, s2.at[0], r2.at[0], right2, z)
    s2[1] = total[s_far, 80:160, :].astype(BF)
    far_l2 = send(8, s2.at[1], r2.at[1], left2, z)
    s2[2] = total[s_right, 80:160, :].astype(BF)
    own_r2 = send(9, s2.at[2], r2.at[2], right2, z)
    s2[3] = total[s_left, 0:80, :].astype(BF)
    own_l2 = send(10, s2.at[3], r2.at[3], left2, z)
    far_r2.wait_recv()
    s2[4] = (total[s_right, 0:80, :] + r2[0].astype(F32)).astype(BF)
    sum_r2 = send(11, s2.at[4], r2.at[4], right2, z)
    far_l2.wait_recv()
    s2[5] = (total[s_left, 80:160, :] + r2[1].astype(F32)).astype(BF)
    sum_l2 = send(12, s2.at[5], r2.at[5], left2, z)
    own_r2.wait_recv()
    own_l2.wait_recv()
    sum_r2.wait_recv()
    top = total[s, 0:80, :] + r2[3].astype(F32) + r2[4].astype(F32)
    sum_l2.wait_recv()
    low = total[s, 80:160, :] + r2[2].astype(F32) + r2[5].astype(F32)
    for t in range(8):
        lanes = slice(t * 128, (t + 1) * 128)
        mine[t, 0:80, :] = top[:, lanes]
        mine[t, 80:160, :] = low[:, lanes]
        s3[t, 0:80, :] = top[:, lanes].astype(BF)
        s3[t, 80:160, :] = low[:, lanes].astype(BF)
    ends = []
    for k in range(1, 8):
        t = lax.rem(z + k, 8)
        ends.append(send(12 + k, s3.at[t], r3.at[k - 1], me, t))
    out = mine[z]
    for k in range(1, 8):
        ends[k - 1].wait_recv()
        out = out + r3[k - 1].astype(F32)
    out_ref[...] = out
    for copy in [far_r, far_l, own_r, own_l, sum_r, sum_l, far_r2, far_l2, own_r2, own_l2, sum_r2, sum_l2] + ends:
        copy.wait_send()


def weight_gradient(x, dk):
    return pl.pallas_call(
        grad_kernel,
        out_shape=(jax.ShapeDtypeStruct((160, 128), F32), jax.ShapeDtypeStruct((256, 1024), BF)),
        in_specs=[VM, VM],
        out_specs=(VM, VM),
        scratch_shapes=[
            pltpu.VMEM((512, 1024), BF),
            pltpu.VMEM((4, 160, 1024), F32),
            pltpu.VMEM((6, 320, 1024), BF),
            pltpu.VMEM((6, 320, 1024), BF),
            pltpu.VMEM((6, 80, 1024), BF),
            pltpu.VMEM((6, 80, 1024), BF),
            pltpu.VMEM((8, 160, 128), BF),
            pltpu.VMEM((7, 160, 128), BF),
            pltpu.VMEM((8, 160, 128), F32),
            pltpu.SemaphoreType.DMA((20,)),
            pltpu.SemaphoreType.DMA((20,)),
        ],
        compiler_params=pltpu.CompilerParams(collective_id=0, has_side_effects=True),
        cost_estimate=pl.CostEstimate(flops=5_400_000_000, bytes_accessed=60_000_000, transcendentals=0),
        name="weight_gradient",
    )(x, dk)


def body(tokens, queries, cotangent, kv_weight, active):
    dp = lax.axis_index("dp")
    z = lax.axis_index("seq")
    core = lax.rem(dp, 2)

    def spread(v):
        v = v.reshape(2, 2, HALF, KVH, GRP * HEAD).transpose(3, 1, 0, 2, 4)
        return v.reshape(8, 2, HALF, GRP * HEAD)

    def swap(v):
        return lax.all_to_all(v, "seq", split_axis=0, concat_axis=0, tiled=True)

    x = tokens[0]
    q_in = swap(spread(queries[0]))
    g_in = swap(spread(cotangent[0]))
    weight = lax.all_gather(kv_weight, "dp", axis=0, tiled=True)

    x_t = x.T.reshape(4, 4, 2, 160, 256)

    def half_of(which):
        return jnp.where(which == 0, x_t[:, :, 0], x_t[:, :, 1].transpose(1, 0, 2, 3)).reshape(4, 640, 256)

    x_mine = half_of(core)
    x_theirs = lax.ppermute(half_of(1 - core), "dp", [(i, i ^ 1) for i in range(32)])
    x_cat = jnp.concatenate([x_mine, x_theirs], axis=2)

    q_in, g_in, weight, x_cat, x = lax.optimization_barrier((q_in, g_in, weight, x_cat, x))
    keyval = jnp.dot(x, weight, preferred_element_type=F32).astype(BF)
    kv_out = keyval.reshape(256, 2, KVH, HEAD).transpose(2, 0, 1, 3).reshape(KVH, 1, 256, 256)
    kv_out = jnp.broadcast_to(kv_out, (KVH, 2, 256, 256)).reshape(8, 256, 256)
    kv_in = swap(kv_out).reshape(NBLK, BLK, 256)
    act = jnp.concatenate([active[0], lax.rem(z, 2)[None].astype(jnp.int32)])
    qg, dkv = attention(act, q_in.reshape(NBLK, HALF, GRP * HEAD), g_in.reshape(NBLK, HALF, GRP * HEAD), kv_in)
    dk = swap(dkv.reshape(8, 256, 256))
    q_back = swap(qg.reshape(8, 2, HALF, GRP * HEAD))
    part, kv_back = weight_gradient(x_cat, dk)
    q_back = q_back.reshape(KVH, 2, 2, HALF, GRP * HEAD).transpose(2, 1, 3, 0, 4).reshape(256, 2560)
    token_grad = lax.dot_general(kv_back, weight, NT, preferred_element_type=F32).astype(BF)
    return (q_back[None], token_grad[None], part)


def solution(mesh):
    in_specs = (
        P("dp", "seq", None),
        P("dp", "seq", None),
        P("dp", "seq", None),
        P("dp", None),
        P("dp", None),
    )
    out_specs = (P("dp", "seq", None), P("dp", "seq", None), P("dp", "seq"))
    return jax.shard_map(body, mesh=mesh, in_specs=in_specs, out_specs=out_specs, check_vma=False)
```

time: 499 us -> 277 us (0.56)
  waiting for transfers between devices: 314 us -> 86.5 us
  Pallas kernels: 0 us -> 84.6 us
  local copies, waits for them, and re-layouts: 68.2 us -> 18.1 us
  matrix products: 44.1 us -> 15.4 us
  other arithmetic: 15.5 us -> 2.99 us
  blocking collectives: 21.6 us -> 33.4 us
    unnamed x6 -> x1, waiting for transfers between devices: 86.9 us -> 0.68 us
    pallas_call x0 -> x2, Pallas kernels: none -> 84.6 us  [the longest x1 53.8 us: weight_gradient(): pl.pallas_call(grad_kernel, out_shape=(jax.ShapeDtypeStruct((160, 128), F...]
    reduce_scatter x2 -> x0, waiting for transfers between devices: 80.7 us -> none  [the longest x1 52.9 us: body(): lax.psum_scatter(kv_terms, 'seq', scatter_dimension=1, tiled=True)]
    all_gather x2 -> x1, waiting for transfers between devices: 68.3 us -> 0.01 us  [body(): weight = lax.all_gather(kv_weight, 'dp', axis=0, tiled=True)]
    unnamed x22 -> x10, local copies, waits for them, and re-layouts: 30 us -> 5.65 us
    dot_general x8 -> x2, matrix products: 35.5 us -> 15.4 us  [the longest x1 8.57 us: body(): lax.dot_general(kv_back, weight, NT, preferred_element_type=F32).astype(BF)]
    all_to_all x1, blocking collectives: 21.6 us -> 33.4 us  [swap(): return lax.all_to_all(v, 'seq', split_axis=0, concat_axis=0, tiled=True)]
    sub x1 -> x0, matrix products: 8.61 us -> none  [body(): exponent = jnp.exp(scores - row_max)]
  transfers between devices with their start and end apart: 9 -> 6, of which waited for: 7 -> 4; matrix products, arithmetic and copies ran while one was open for 10% -> 8% of each run, Pallas kernels for 0% -> 19%
where the time goes in v1:
time: 277 us; the launch traced here: 276 us
  waiting for transfers between devices  86.5 us (31%)
  Pallas kernels  84.6 us (31%)
  blocking collectives  33.4 us (12%)
  starting transfers between devices  20.7 us (7%)
  local copies, waits for them, and re-layouts  18.1 us (7%)
  matrix products  15.4 us (6%)
  between operations  14.2 us (5%)
  other arithmetic  2.99 us (1%)
    all_to_all x4, waiting for transfers between devices, swap(): return lax.all_to_all(v, 'seq', split_axis=0, concat_axis=0, tiled=True)  82.5 us
    pallas_call x1, Pallas kernels, weight_gradient(): pl.pallas_call(grad_kernel, out_shape=(jax.ShapeDtypeStruct((160, 128), F...  53.8 us
    all_to_all x1, blocking collectives, swap(): return lax.all_to_all(v, 'seq', split_axis=0, concat_axis=0, tiled=True)  33.4 us
    pallas_call x1, Pallas kernels, attention(): pl.pallas_call(attention_kernel, out_shape=(jax.ShapeDtypeStruct(q.shape,...  30.8 us
    all_to_all x4, starting transfers between devices, swap(): return lax.all_to_all(v, 'seq', split_axis=0, concat_axis=0, tiled=True)  20.4 us
    dot_general x1, matrix products, body(): lax.dot_general(kv_back, weight, NT, preferred_element_type=F32).astype(BF)  8.57 us
    dot_general x1, matrix products, body(): keyval = jnp.dot(x, weight, preferred_element_type=F32).astype(BF)  6.87 us
    unnamed x10, local copies, waits for them, and re-layouts  5.65 us
  transfers between devices with their start and end apart: 6, of which 4 were waited for; matrix products, arithmetic and copies ran while one was open for 8% of the time, Pallas kernels for 19%

profile of v1, /device:TPU:2, one launch (start us, length us, event | category | flops | bytes accessed | tf_op | source)
XLA Modules:
  0.0 275.9 jit_solution(894566824689581188)
XLA Ops:
  7.2 0.0 all-gather.2.cloned.1.call-start
  7.2 0.7 all-gather.2.cloned.1.call-update
  7.9 2.7 reshape_squeeze.6
  10.6 1.3 copy.13
  11.9 8.5 %all-to-all-start = ((bf16[8,2,64,640]{3,2,1,0:T(8,128)(2,1)}), bf16[8,2,64,640]{3,2,1,0:T(8,128)(2,1)S(1)}, u32[]{:S(2)}, u32[]{:S(2)}) async-start(bf16[8,2,64,640]{3,2,1,0:T(8,128)(2,1)} %bitcast.3), calls=%async_computation | async-start | bytes 2621440 | tf_op jit(solution)/shard_map/all_to_all | solution.py:248
  20.3 2.7 reshape_squeeze.7
  23.0 1.3 copy.14
  24.3 30.5 %all-to-all-done = bf16[8,2,64,640]{3,2,1,0:T(8,128)(2,1)S(1)} async-done(((bf16[8,2,64,640]{3,2,1,0:T(8,128)(2,1)}), bf16[8,2,64,640]{3,2,1,0:T(8,128)(2,1)S(1)}, u32[]{:S(2)}, u32[]{:S(2)}) %all-to-all-start) | async-done | bytes 1310752 | tf_op jit(solution)/shard_map/all_to_all | solution.py:248
  54.8 0.0 copy-start
  54.8 1.1 copy-done
  55.8 4.3 %all-to-all-start.1 = ((bf16[8,2,64,640]{3,2,1,0:T(8,128)(2,1)}), bf16[8,2,64,640]{3,2,1,0:T(8,128)(2,1)}, u32[]{:S(2)}, u32[]{:S(2)}) async-start(bf16[8,2,64,640]{3,2,1,0:T(8,128)(2,1)} %bitcast.5), calls=%async_computation.1 | async-start | bytes 2621440 | tf_op jit(solution)/shard_map/all_to_all | solution.py:248
  60.1 3.0 %copy.15 = bf16[1,256,5120]{1,2,0:T(8,128)(2,1)S(1)} copy(bf16[1,256,5120]{2,1,0:T(8,128)(2,1)} %param.5) | data formatting | bytes 5242880 | tf_op args[0]
  63.1 0.6 broadcast_select_fusion.1
  63.7 0.1 copy.18
  63.8 0.2 collective-permute-start
  64.1 0.1 copy.17
  64.2 3.3 %collective-permute-done = bf16[4,640,256]{2,1,0:T(8,128)(2,1)S(1)} collective-permute-done((bf16[4,640,256]{2,1,0:T(8,128)(2,1)S(1)}, bf16[4,640,256]{2,1,0:T(8,128)(2,1)S(1)}, u32[]{:S(2)}, u32[]{:S(2)}) %collective-permute-start) | collective-permute-done | bytes 1310752 | tf_op jit(solution)/shard_map/ppermute | solution.py:261
  67.5 1.7 pad_maximum_fusion.x_ref
  69.2 25.7 %all-to-all-done.1 = bf16[8,2,64,640]{3,2,1,0:T(8,128)(2,1)} async-done(((bf16[8,2,64,640]{3,2,1,0:T(8,128)(2,1)}), bf16[8,2,64,640]{3,2,1,0:T(8,128)(2,1)}, u32[]{:S(2)}, u32[]{:S(2)}) %all-to-all-start.1) | async-done | bytes 1310752 | tf_op jit(solution)/shard_map/all_to_all | solution.py:248
  94.9 0.0 all-gather.2.cloned.1.call-done
  94.9 6.9 %convolution_convert_fusion.1 = bf16[256,1024]{1,0:T(8,128)(2,1)S(1)} fusion(bf16[256,5120]{0,1:T(8,128)(2,1)S(1)} %bitcast.47, bf16[5120,1024]{1,0:T(8,128)(2,1)} %all-gather.2.cloned.1.call-done), kind=kOutput, calls=%fused_computation.8 | convolution fusion | flops 2684616704 | bytes 13631488 | tf_op jit(solution)/shard_map/dot_general | solution.py:265
  101.8 0.4 reshape.54
  102.2 0.3 copy.19
  102.5 0.2 copy.20
  102.7 1.0 broadcast_in_dim.15
  103.8 0.0 copy-start.3
  103.8 3.9 %all-to-all-start.2 = ((bf16[8,256,256]{2,1,0:T(8,128)(2,1)}), bf16[8,256,256]{2,1,0:T(8,128)(2,1)S(1)}, u32[]{:S(2)}, u32[]{:S(2)}) async-start(bf16[8,256,256]{2,1,0:T(8,128)(2,1)} %bitcast.21), calls=%async_computation.2 | async-start | bytes 2097152 | tf_op jit(solution)/shard_map/all_to_all | solution.py:248
  107.6 0.0 copy-done.3
  107.6 0.7 pad_add_fusion.act
  108.3 26.3 %all-to-all-done.2 = bf16[8,256,256]{2,1,0:T(8,128)(2,1)S(1)} async-done(((bf16[8,256,256]{2,1,0:T(8,128)(2,1)}), bf16[8,256,256]{2,1,0:T(8,128)(2,1)S(1)}, u32[]{:S(2)}, u32[]{:S(2)}) %all-to-all-start.2) | async-done | bytes 1048608 | tf_op jit(solution)/shard_map/all_to_all | solution.py:248
  134.6 0.0 copy-start.1
  134.6 1.0 copy-done.1
  135.6 30.8 %attention.1 = (bf16[16,64,640]{2,1,0:T(8,128)(2,1)}, bf16[16,128,256]{2,1,0:T(8,128)(2,1)}) custom-call(s32[9]{0:T(128)} %pad_add_fusion.act, bf16[16,64,640]{2,1,0:T(8,128)(2,1)} %bitcast.53, bf16[16,64,640]{2,1,0:T(8,128)(2,1)} %bitcast.18.g_ref, bf16[16,128,256]{2,1,0:T(8,128)(2,1)} %bitcast.54), custom_call_target="tpu_custom_call" | custom-call | tf_op jit(solution)/shard_map/attention/pallas_call | solution.py:79
  166.4 33.4 %all_to_all.25.dk_ref = bf16[8,256,256]{2,1,0:T(8,128)(2,1)} all-to-all(bf16[8,256,256]{2,1,0:T(8,128)(2,1)} %bitcast.57), channel_id=1, replica_groups=mesh['dp'=32,'seq'=8] {'seq'}, dimensions={0} | all-to-all | bytes 2097152 | tf_op jit(solution)/shard_map/all_to_all | solution.py:248
  199.8 3.8 %all-to-all-start.3 = ((bf16[8,2,64,640]{3,2,1,0:T(8,128)(2,1)}), bf16[8,2,64,640]{3,2,1,0:T(8,128)(2,1)S(1)}, u32[]{:S(2)}, u32[]{:S(2)}) async-start(bf16[8,2,64,640]{3,2,1,0:T(8,128)(2,1)} %bitcast.23), calls=%async_computation.3 | async-start | bytes 2621440 | tf_op jit(solution)/shard_map/all_to_all | solution.py:248
  203.6 53.8 %weight_gradient.1 = (f32[160,128]{1,0:T(8,128)}, bf16[256,1024]{1,0:T(8,128)(2,1)}) custom-call(bf16[4,640,512]{2,1,0:T(8,128)(2,1)} %pad_maximum_fusion.x_ref, bf16[8,256,256]{2,1,0:T(8,128)(2,1)} %all_to_all.25.dk_ref), custom_call_target="tpu_custom_call" | custom-call | flops 5400000000 | bytes 60000000 | tf_op jit(solution)/shard_map/weight_gradient/pallas_call | solution.py:214
  257.4 8.6 %fusion = bf16[1,256,5120]{2,1,0:T(8,128)(2,1)} fusion(bf16[256,1024]{1,0:T(8,128)(2,1)} %get-tuple-element.19, bf16[5120,1024]{1,0:T(8,128)(2,1)} %all-gather.2.cloned.1.call-done), kind=kOutput, calls=%fused_computation.1 | convolution fusion | flops 2685665280 | bytes 13631488 | tf_op jit(solution)/shard_map/dot_general | solution.py:275
  266.0 0.0 all-to-all-done.3
  266.0 1.0 copy.29
  267.0 0.0 copy-start.2
  267.0 1.4 broadcast_in_dim_reshape.3
  268.4 0.0 copy-done.2
  268.4 0.6 copy.31
Async XLA Ops:
  7.2 87.7 %all-gather.2.cloned.1.call-start = ((), (), s32[]{:S(2)}) async-start(), calls=%async_computation.5 | async-start | bytes 10813440 | tf_op jit(solution)/shard_map/all_gather | solution.py:253
  11.9 42.9 %all-to-all-start = ((bf16[8,2,64,640]{3,2,1,0:T(8,128)(2,1)}), bf16[8,2,64,640]{3,2,1,0:T(8,128)(2,1)S(1)}, u32[]{:S(2)}, u32[]{:S(2)}) async-start(bf16[8,2,64,640]{3,2,1,0:T(8,128)(2,1)} %bitcast.3), calls=%async_computation | async-start | bytes 2621440 | tf_op jit(solution)/shard_map/all_to_all | solution.py:248
  54.8 1.1 copy-start
  55.8 39.1 %all-to-all-start.1 = ((bf16[8,2,64,640]{3,2,1,0:T(8,128)(2,1)}), bf16[8,2,64,640]{3,2,1,0:T(8,128)(2,1)}, u32[]{:S(2)}, u32[]{:S(2)}) async-start(bf16[8,2,64,640]{3,2,1,0:T(8,128)(2,1)} %bitcast.5), calls=%async_computation.1 | async-start | bytes 2621440 | tf_op jit(solution)/shard_map/all_to_all | solution.py:248
  63.8 3.6 %collective-permute-start = (bf16[4,640,256]{2,1,0:T(8,128)(2,1)S(1)}, bf16[4,640,256]{2,1,0:T(8,128)(2,1)S(1)}, u32[]{:S(2)}, u32[]{:S(2)}) collective-permute-start(bf16[4,640,256]{2,1,0:T(8,128)(2,1)S(1)} %bitcast.56), channel_id=1, source_target_pairs={{0,8},{8,0},{16,24},{24,16},{32,40},{40,32},{48,56},{56,48},{64,72... | collective-permute-start | bytes 3932168 | tf_op jit(solution)/shard_map/ppermute | solution.py:261
  103.8 3.9 %copy-start.3 = (s32[1,8]{1,0:T(1,128)S(1)}, s32[1,8]{1,0:T(1,128)}, u32[]{:S(2)}) copy-start(s32[1,8]{1,0:T(1,128)} %param.9) | copy-start | bytes 100
  103.8 30.9 %all-to-all-start.2 = ((bf16[8,256,256]{2,1,0:T(8,128)(2,1)}), bf16[8,256,256]{2,1,0:T(8,128)(2,1)S(1)}, u32[]{:S(2)}, u32[]{:S(2)}) async-start(bf16[8,256,256]{2,1,0:T(8,128)(2,1)} %bitcast.21), calls=%async_computation.2 | async-start | bytes 2097152 | tf_op jit(solution)/shard_map/all_to_all | solution.py:248
  134.6 1.0 copy-start.1
  199.8 66.1 %all-to-all-start.3 = ((bf16[8,2,64,640]{3,2,1,0:T(8,128)(2,1)}), bf16[8,2,64,640]{3,2,1,0:T(8,128)(2,1)S(1)}, u32[]{:S(2)}, u32[]{:S(2)}) async-start(bf16[8,2,64,640]{3,2,1,0:T(8,128)(2,1)} %bitcast.23), calls=%async_computation.3 | async-start | bytes 2621440 | tf_op jit(solution)/shard_map/all_to_all | solution.py:248
  267.0 1.4 copy-start.2
Sparse Core Ops, SparseCore 0:
  10.5 65.5 all-gather.1

commit v2 on v1

--- a/solution.py
+++ b/solution.py
@@ -30,7 +30,6 @@
         kc[j * BLK : (j + 1) * BLK, :] = block[:, :HEAD]
         vc[j * BLK : (j + 1) * BLK, :] = block[:, HEAD:]
     qg_ref[...] = jnp.zeros_like(qg_ref)
-    dkv_ref[...] = jnp.zeros_like(dkv_ref)
     step = 32
     for a in reversed(range(NACT)):
         n = (a + 1) * BLK
@@ -69,16 +68,15 @@
             dkt[:, :n] += dk
             dvt[:, :n] += dv
     for j in range(NACT):
-        b = act[j]
-        dkv_ref[b, :, :HEAD] = dkt[:, j * BLK : (j + 1) * BLK].T.astype(BF)
-        dkv_ref[b, :, HEAD:] = dvt[:, j * BLK : (j + 1) * BLK].T.astype(BF)
+        dkv_ref[0, j] = dkt[:, j * BLK : (j + 1) * BLK].T
+        dkv_ref[1, j] = dvt[:, j * BLK : (j + 1) * BLK].T
 
 
 def attention(act, q, g, kv):
     n = NACT * BLK
     return pl.pallas_call(
         attention_kernel,
-        out_shape=(jax.ShapeDtypeStruct(q.shape, BF), jax.ShapeDtypeStruct(kv.shape, BF)),
+        out_shape=(jax.ShapeDtypeStruct(q.shape, BF), jax.ShapeDtypeStruct((2, NACT, BLK, HEAD), F32)),
         in_specs=[pl.BlockSpec(memory_space=pltpu.SMEM), VM, VM, VM],
         out_specs=(VM, VM),
         scratch_shapes=[
@@ -95,14 +93,48 @@
     )(act, q, g, kv)
 
 
-def grad_kernel(x_ref, dk_ref, out_ref, kvb_ref, kv2, total, s1, r1, s2, r2, s3, r3, mine, ssem, rsem):
+def ring_places():
     me = lax.axis_index("dp")
-    z = lax.axis_index("seq")
     c = lax.rem(me, 2)
     cy = lax.rem(me // 2, 4)
     cx = me // 8
-    f = cx + (cy - cx) * c
-    s = cy + (cx - cy) * c
+    return me, c, cx + (cy - cx) * c, cy + (cx - cy) * c
+
+
+def greet(peers, me, z):
+    barrier = pltpu.get_barrier_semaphore()
+    for peer in peers:
+        pl.semaphore_signal(barrier, inc=1, device_id=(peer, z), device_id_type=MESH)
+    for k in range(1, 8):
+        pl.semaphore_signal(barrier, inc=1, device_id=(me, lax.rem(z + k, 8)), device_id_type=MESH)
+    return barrier
+
+
+def remote(src, dst, ssem, rsem, dev, seq):
+    copy = pltpu.make_async_remote_copy(
+        src_ref=src, dst_ref=dst, send_sem=ssem, recv_sem=rsem, device_id=(dev, seq), device_id_type=MESH
+    )
+    copy.start()
+    return copy
+
+
+def local(src, dst, sem):
+    copy = pltpu.make_async_copy(src, dst, sem)
+    copy.start()
+    return copy
+
+
+def seq_lanes(t):
+    return pl.ds(pl.multiple_of((t // 2) * (GRP * HEAD), 128), GRP * HEAD)
+
+
+def seq_rows(t):
+    return pl.ds(pl.multiple_of(lax.rem(t, 2) * HALF, HALF), HALF)
+
+
+def gather_kernel(q_ref, g_ref, w_in, x_ref, q_out, g_out, kv_out, w_out, w, kvb, acc, zs, zr, ws, wr, ls):
+    z = lax.axis_index("seq")
+    me, c, f, s = ring_places()
 
     def device(ff, ss):
         return ff * (8 - 6 * c) + ss * (2 + 6 * c) + c
@@ -112,30 +144,175 @@
     s_right, s_left, s_far = lax.rem(s + 1, 4), lax.rem(s + 3, 4), lax.rem(s + 2, 4)
     right1, left1 = device(f_right, s), device(f_left, s)
     right2, left2 = device(f, s_right), device(f, s_left)
-
-    barrier = pltpu.get_barrier_semaphore()
-    for peer in (partner, right1, left1, right2, left2):
-        pl.semaphore_signal(barrier, inc=1, device_id=(peer, z), device_id_type=MESH)
-    for k in range(1, 8):
-        pl.semaphore_signal(barrier, inc=1, device_id=(me, lax.rem(z + k, 8)), device_id_type=MESH)
+    barrier = greet((partner, right1, left1, right2, left2), me, z)
+    locals_ = [local(w_in, w.at[me], ls.at[0])]
+    locals_.append(local(q_ref.at[:, seq_rows(z), seq_lanes(z)], q_out.at[z], ls.at[1]))
+    locals_.append(local(g_ref.at[:, seq_rows(z), seq_lanes(z)], g_out.at[z], ls.at[2]))
+    locals_[0].wait()
+    pl.semaphore_wait(barrier, 12)
+
+    count = [0]
+    rings = []
+
+    def push(src, dev):
+        n = count[0]
+        count[0] += 1
+        copy = remote(src, src, ws.at[n], wr.at[n], dev, z)
+        rings.append(copy)
+        return copy
+
+    def half(i, p):
+        return w.at[i, p * 80 : (p + 1) * 80]
+
+    a_right, a_left = push(w.at[me], right1), push(w.at[me], left1)
+    second = [(f, push(w.at[me], right2), push(w.at[me], left2))]
+    chip = [push(w.at[me], partner)]
+    ends = []
+    for ref, out, base in ((q_ref, q_out, 0), (g_ref, g_out, 7)):
+        for k in (1, 7, 2, 6, 3, 5, 4):
+            t = lax.rem(z + k, 8)
+            ends.append(
+                remote(ref.at[:, seq_rows(t), seq_lanes(t)], out.at[z], zs.at[base + k - 1], zr.at[base + k - 1], me, t)
+            )
+
+    def ready(ff, ss):
+        i = device(ff, ss)
+        chip.append(push(w.at[i], partner))
+        return i
+
+    a_right.wait_recv()
+    i = device(f_left, s)
+    far_a = push(half(i, 0), right1)
+    second.append((f_left, push(w.at[i], right2), push(w.at[i], left2)))
+    ready(f_left, s)
+    a_left.wait_recv()
+    i = device(f_right, s)
+    far_b = push(half(i, 1), left1)
+    second.append((f_right, push(w.at[i], right2), push(w.at[i], left2)))
+    ready(f_right, s)
+    thirds = []
+
+    def forward(entry):
+        ff, to_right, to_left = entry
+        to_right.wait_recv()
+        i = ready(ff, s_left)
+        one = push(half(i, 0), right2)
+        to_left.wait_recv()
+        i = ready(ff, s_right)
+        thirds.append((ff, one, push(half(i, 1), left2)))
+
+    forward(second[0])
+    far_a.wait_recv()
+    far_b.wait_recv()
+    i = ready(f_far, s)
+    second.append((f_far, push(w.at[i], right2), push(w.at[i], left2)))
+    for entry in second[1:]:
+        forward(entry)
+    for ff, one, two in thirds:
+        one.wait_recv()
+        two.wait_recv()
+        ready(ff, s_far)
+    for copy in chip:
+        copy.wait_recv()
+    locals_.append(local(w, w_out, ls.at[3]))
+
+    def tile(j):
+        block = w[4 * j : 4 * j + 4].reshape(640, 1024)
+        return jnp.dot(x_ref[:, j * 640 : (j + 1) * 640], block, preferred_element_type=F32)
+
+    acc[...] = tile(0)
+    for j in range(1, 8):
+        acc[...] += tile(j)
     for h in range(KVH):
-        for part in range(2):
-            lanes = slice(part * HEAD, (part + 1) * HEAD)
-            both = dk_ref[2 * h, :, lanes].astype(F32) + dk_ref[2 * h + 1, :, lanes].astype(F32)
-            kv2[0:256, (part * KVH + h) * HEAD : (part * KVH + h + 1) * HEAD] = both.astype(BF)
+        kvb[h, :, :HEAD] = acc[:, h * HEAD : (h + 1) * HEAD].astype(BF)
+        kvb[h, :, HEAD:] = acc[:, (KVH + h) * HEAD : (KVH + h + 1) * HEAD].astype(BF)
+    locals_.append(local(kvb.at[z // 2], kv_out.at[z], ls.at[4]))
+    for k in (1, 7, 2, 6, 3, 5, 4):
+        t = lax.rem(z + k, 8)
+        ends.append(remote(kvb.at[t // 2], kv_out.at[z], zs.at[13 + k], zr.at[13 + k], me, t))
+    for copy in rings:
+        copy.wait_send()
+    for copy in ends:
+        copy.wait()
+    for copy in locals_[1:]:
+        copy.wait()
+
+
+ANY = pl.BlockSpec(memory_space=pl.ANY)
+
+
+def gather(q, g, w, x):
+    piece = jax.ShapeDtypeStruct((8, 2, HALF, GRP * HEAD), BF)
+    return pl.pallas_call(
+        gather_kernel,
+        out_shape=(
+            piece,
+            piece,
+            jax.ShapeDtypeStruct((8, 256, 256), BF),
+            jax.ShapeDtypeStruct((32, 160, 1024), BF),
+        ),
+        in_specs=[ANY, ANY, ANY, VM],
+        out_specs=(ANY, ANY, ANY, ANY),
+        scratch_shapes=[
+            pltpu.VMEM((32, 160, 1024), BF),
+            pltpu.VMEM((4, 256, 256), BF),
+            pltpu.VMEM((256, 1024), F32),
+            pltpu.SemaphoreType.DMA((21,)),
+            pltpu.SemaphoreType.DMA((21,)),
+            pltpu.SemaphoreType.DMA((36,)),
+            pltpu.SemaphoreType.DMA((36,)),
+            pltpu.SemaphoreType.DMA((5,)),
+        ],
+        compiler_params=pltpu.CompilerParams(collective_id=1, has_side_effects=True),
+        name="gather",
+    )(q, g, w, x)
+
+
+def grad_kernel(
+    inv, x_ref, dk_ref, qg_ref, out_ref, kvb_ref, q_out, kv2, pair, summed, pad, got, total, s1, r1, s2, r2, s3, r3, mine, ssem, rsem, zs, zr, ls
+):
+    z = lax.axis_index("seq")
+    me, c, f, s = ring_places()
+
+    def device(ff, ss):
+        return ff * (8 - 6 * c) + ss * (2 + 6 * c) + c
+
+    partner = me + 1 - 2 * c
+    f_right, f_left, f_far = lax.rem(f + 1, 4), lax.rem(f + 3, 4), lax.rem(f + 2, 4)
+    s_right, s_left, s_far = lax.rem(s + 1, 4), lax.rem(s + 3, 4), lax.rem(s + 2, 4)
+    right1, left1 = device(f_right, s), device(f_left, s)
+    right2, left2 = device(f, s_right), device(f, s_left)
+    barrier = greet((partner, right1, left1, right2, left2), me, z)
+    half = lax.rem(z, 2)
     pl.semaphore_wait(barrier, 12)
 
+    trade = remote(dk_ref.at[1 - half], pair, zs.at[14], zr.at[14], me, z + 1 - 2 * half)
+    summed[NACT] = jnp.zeros((BLK, HEAD), BF)
+    trade.wait_recv()
+    summed[0:NACT] = (dk_ref[half] + pair[...]).astype(BF)
+    for b in range(NBLK):
+        pad[b] = summed[inv[b]]
+    own = [local(pad.at[pl.ds(2 * z, 2)], got.at[z], ls.at[0])]
+    spread, back = [], []
+    for k in (1, 7, 2, 6, 3, 5, 4):
+        t = lax.rem(z + k, 8)
+        spread.append(remote(pad.at[pl.ds(2 * t, 2)], got.at[z], zs.at[k - 1], zr.at[k - 1], me, t))
+    own.append(local(qg_ref.at[z], q_out.at[:, seq_rows(z), seq_lanes(z)], ls.at[1]))
+    for k in (1, 7, 2, 6, 3, 5, 4):
+        t = lax.rem(z + k, 8)
+        back.append(
+            remote(qg_ref.at[t], q_out.at[:, seq_rows(z), seq_lanes(z)], zs.at[6 + k], zr.at[6 + k], me, t)
+        )
+    own[0].wait()
+    for copy in spread:
+        copy.wait_recv()
+    for j in range(8):
+        lanes = slice(((j % 2) * KVH + j // 2) * HEAD, ((j % 2) * KVH + j // 2 + 1) * HEAD)
+        kv2[0:128, lanes] = got[j, 0]
+        kv2[128:256, lanes] = got[j, 1]
+
     def send(index, src, dst, dev, seq):
-        copy = pltpu.make_async_remote_copy(
-            src_ref=src,
-            dst_ref=dst,
-            send_sem=ssem.at[index],
-            recv_sem=rsem.at[index],
-            device_id=(dev, seq),
-            device_id_type=MESH,
-        )
-        copy.start()
-        return copy
+        return remote(src, dst, ssem.at[index], rsem.at[index], dev, seq)
 
     swap = send(0, kv2.at[0:256], kv2.at[256:512], partner, z)
     kvb_ref[...] = kv2[0:256, :]
@@ -206,18 +383,29 @@
         ends[k - 1].wait_recv()
         out = out + r3[k - 1].astype(F32)
     out_ref[...] = out
-    for copy in [far_r, far_l, own_r, own_l, sum_r, sum_l, far_r2, far_l2, own_r2, own_l2, sum_r2, sum_l2] + ends:
+    for copy in [far_r, far_l, own_r, own_l, sum_r, sum_l, far_r2, far_l2, own_r2, own_l2, sum_r2, sum_l2, trade] + ends + spread:
         copy.wait_send()
-
-
-def weight_gradient(x, dk):
+    own[1].wait()
+    for copy in back:
+        copy.wait()
+
+
+def weight_gradient(inv, x, dk, qg):
     return pl.pallas_call(
         grad_kernel,
-        out_shape=(jax.ShapeDtypeStruct((160, 128), F32), jax.ShapeDtypeStruct((256, 1024), BF)),
-        in_specs=[VM, VM],
-        out_specs=(VM, VM),
+        out_shape=(
+            jax.ShapeDtypeStruct((160, 128), F32),
+            jax.ShapeDtypeStruct((256, 1024), BF),
+            jax.ShapeDtypeStruct((2, BLK, 2560), BF),
+        ),
+        in_specs=[pl.BlockSpec(memory_space=pltpu.SMEM), VM, VM, ANY],
+        out_specs=(VM, VM, ANY),
         scratch_shapes=[
             pltpu.VMEM((512, 1024), BF),
+            pltpu.VMEM((NACT, BLK, HEAD), F32),
+            pltpu.VMEM((NACT + 1, BLK, HEAD), BF),
+            pltpu.VMEM((NBLK, BLK, HEAD), BF),
+            pltpu.VMEM((8, 2, BLK, HEAD), BF),
             pltpu.VMEM((4, 160, 1024), F32),
             pltpu.VMEM((6, 320, 1024), BF),
             pltpu.VMEM((6, 320, 1024), BF),
@@ -228,52 +416,40 @@
             pltpu.VMEM((8, 160, 128), F32),
             pltpu.SemaphoreType.DMA((20,)),
             pltpu.SemaphoreType.DMA((20,)),
+            pltpu.SemaphoreType.DMA((15,)),
+            pltpu.SemaphoreType.DMA((15,)),
+            pltpu.SemaphoreType.DMA((2,)),
         ],
         compiler_params=pltpu.CompilerParams(collective_id=0, has_side_effects=True),
-        cost_estimate=pl.CostEstimate(flops=5_400_000_000, bytes_accessed=60_000_000, transcendentals=0),
         name="weight_gradient",
-    )(x, dk)
+    )(inv, x, dk, qg)
 
 
 def body(tokens, queries, cotangent, kv_weight, active):
     dp = lax.axis_index("dp")
     z = lax.axis_index("seq")
     core = lax.rem(dp, 2)
-
-    def spread(v):
-        v = v.reshape(2, 2, HALF, KVH, GRP * HEAD).transpose(3, 1, 0, 2, 4)
-        return v.reshape(8, 2, HALF, GRP * HEAD)
-
-    def swap(v):
-        return lax.all_to_all(v, "seq", split_axis=0, concat_axis=0, tiled=True)
-
     x = tokens[0]
-    q_in = swap(spread(queries[0]))
-    g_in = swap(spread(cotangent[0]))
-    weight = lax.all_gather(kv_weight, "dp", axis=0, tiled=True)
-
     x_t = x.T.reshape(4, 4, 2, 160, 256)
 
     def half_of(which):
         return jnp.where(which == 0, x_t[:, :, 0], x_t[:, :, 1].transpose(1, 0, 2, 3)).reshape(4, 640, 256)
 
-    x_mine = half_of(core)
     x_theirs = lax.ppermute(half_of(1 - core), "dp", [(i, i ^ 1) for i in range(32)])
-    x_cat = jnp.concatenate([x_mine, x_theirs], axis=2)
-
-    q_in, g_in, weight, x_cat, x = lax.optimization_barrier((q_in, g_in, weight, x_cat, x))
-    keyval = jnp.dot(x, weight, preferred_element_type=F32).astype(BF)
-    kv_out = keyval.reshape(256, 2, KVH, HEAD).transpose(2, 0, 1, 3).reshape(KVH, 1, 256, 256)
-    kv_out = jnp.broadcast_to(kv_out, (KVH, 2, 256, 256)).reshape(8, 256, 256)
-    kv_in = swap(kv_out).reshape(NBLK, BLK, 256)
+    x_cat = jnp.concatenate([half_of(core), x_theirs], axis=2)
     act = jnp.concatenate([active[0], lax.rem(z, 2)[None].astype(jnp.int32)])
-    qg, dkv = attention(act, q_in.reshape(NBLK, HALF, GRP * HEAD), g_in.reshape(NBLK, HALF, GRP * HEAD), kv_in)
-    dk = swap(dkv.reshape(8, 256, 256))
-    q_back = swap(qg.reshape(8, 2, HALF, GRP * HEAD))
-    part, kv_back = weight_gradient(x_cat, dk)
-    q_back = q_back.reshape(KVH, 2, 2, HALF, GRP * HEAD).transpose(2, 1, 3, 0, 4).reshape(256, 2560)
-    token_grad = lax.dot_general(kv_back, weight, NT, preferred_element_type=F32).astype(BF)
-    return (q_back[None], token_grad[None], part)
+    same = active[0][None, :] == jnp.arange(NBLK, dtype=jnp.int32)[:, None]
+    inv = NACT - jnp.sum(jnp.where(same, NACT - jnp.arange(NACT, dtype=jnp.int32)[None, :], 0), axis=1)
+
+    queries, cotangent, x_cat = lax.optimization_barrier((queries, cotangent, x_cat))
+    q_in, g_in, kv_in, weight = gather(
+        queries.reshape(2, BLK, 2560), cotangent.reshape(2, BLK, 2560), kv_weight, x
+    )
+    rows = (NBLK, HALF, GRP * HEAD)
+    qg, dkv = attention(act, q_in.reshape(rows), g_in.reshape(rows), kv_in.reshape(NBLK, BLK, 256))
+    part, kv_back, q_back = weight_gradient(inv, x_cat, dkv, qg.reshape(8, 2, HALF, GRP * HEAD))
+    token_grad = lax.dot_general(kv_back, weight.reshape(5120, 1024), NT, preferred_element_type=F32).astype(BF)
+    return (q_back.reshape(1, 256, 2560), token_grad[None], part)
 
 
 def solution(mesh):

time: 277 us -> 226 us (0.82)
  Pallas kernels: 84.6 us -> 202 us
  waiting for transfers between devices: 86.5 us -> 0.81 us
  blocking collectives: 33.4 us -> 0 us
  starting transfers between devices: 20.7 us -> 0.01 us
  between operations: 14.2 us -> 0.7 us
  local copies, waits for them, and re-layouts: 18.1 us -> 7.09 us
  matrix products: 15.4 us -> 8.65 us
  other arithmetic: 2.99 us -> 5.86 us
    pallas_call x0 -> x1, Pallas kernels: none -> 91.1 us  [gather(): pl.pallas_call(gather_kernel, out_shape=(piece, piece, jax.ShapeDtypeStru...]
    all_to_all x4 -> x0, waiting for transfers between devices: 82.5 us -> none  [swap(): return lax.all_to_all(v, 'seq', split_axis=0, concat_axis=0, tiled=True)]
    all_to_all x1 -> x0, blocking collectives: 33.4 us -> none  [swap(): return lax.all_to_all(v, 'seq', split_axis=0, concat_axis=0, tiled=True)]
    pallas_call x1, Pallas kernels: 53.8 us -> 80.5 us  [weight_gradient(): pl.pallas_call(grad_kernel, out_shape=(jax.ShapeDtypeStruct((160, 128), F...]
    all_to_all x4 -> x0, starting transfers between devices: 20.4 us -> none  [swap(): return lax.all_to_all(v, 'seq', split_axis=0, concat_axis=0, tiled=True)]
    dot_general x2 -> x1, matrix products: 15.4 us -> 8.65 us  [body(): lax.dot_general(kv_back, weight.reshape(5120, 1024), NT, preferred_elemen...]
    another operation x3 -> x0, local copies, waits for them, and re-layouts: 6.76 us -> none  [the longest x2 5.4 us: spread(): v = v.reshape(2, 2, HALF, KVH, GRP * HEAD).transpose(3, 1, 0, 2, 4)]
  transfers between devices with their start and end apart: 6 -> 1, of which waited for: 4 -> 1; matrix products, arithmetic and copies ran while one was open for 8% -> 1% of each run, Pallas kernels for 19% -> 0%
where the time goes in v2:
time: 226 us; the launch traced here: 225 us
  Pallas kernels  202 us (89%)
  matrix products  8.65 us (4%)
  local copies, waits for them, and re-layouts  7.09 us (3%)
  other arithmetic  5.86 us (3%)
    pallas_call x1, Pallas kernels, gather(): pl.pallas_call(gather_kernel, out_shape=(piece, piece, jax.ShapeDtypeStru...  91.1 us
    pallas_call x1, Pallas kernels, weight_gradient(): pl.pallas_call(grad_kernel, out_shape=(jax.ShapeDtypeStruct((160, 128), F...  80.5 us
    pallas_call x1, Pallas kernels, attention(): pl.pallas_call(attention_kernel, out_shape=(jax.ShapeDtypeStruct(q.shape,...  30.8 us
    dot_general x1, matrix products, body(): lax.dot_general(kv_back, weight.reshape(5120, 1024), NT, preferred_elemen...  8.65 us
  transfers between devices with their start and end apart: 1, of which 1 were waited for; matrix products, arithmetic and copies ran while one was open for 1% of the time, Pallas kernels for 0%

profile of v2, /device:TPU:2, one launch (start us, length us, event | category | flops | bytes accessed | tf_op | source)
XLA Modules:
  0.0 225.4 jit_solution(963097559443391255)
XLA Ops:
  0.6 3.0 %copy.14 = bf16[5120,256]{1,0:T(8,128)(2,1)S(1)} copy(bf16[5120,256]{0,1:T(8,128)(2,1)} %bitcast.34) | data formatting | bytes 5242880 | tf_op jit(solution)/shard_map/transpose | solution.py:433
  3.6 1.6 broadcast_select_fusion.1
  5.2 0.0 copy-start
  5.2 1.1 copy.17
  6.4 0.0 collective-permute-start
  6.4 0.6 copy-done
  7.0 0.0 copy-start.3
  7.0 0.1 copy.16
  7.1 0.5 copy-done.3
  7.7 0.7 pad_add_fusion.act
  8.3 0.1 select_reduce_fusion
  8.4 0.5 broadcast_subtract_fusion.inv
  8.9 0.8 collective-permute-done
  9.7 3.0 %pad_maximum_fusion.x_ref = bf16[4,640,512]{2,1,0:T(8,128)(2,1)} fusion(bf16[4,640,256]{2,1,0:T(8,128)(2,1)} %collective-permute-done, bf16[4,640,256]{2,1,0:T(8,128)(2,1)S(1)} %bitcast.37), kind=kLoop, calls=%fused_computation.2 | loop fusion | flops 5242880 | bytes 5242880 | tf_op jit(solution)/shard_map/concatenate | solution.py:439
  12.7 91.1 %gather.1 = (bf16[8,2,64,640]{3,2,1,0:T(8,128)(2,1)}, bf16[8,2,64,640]{3,2,1,0:T(8,128)(2,1)}, bf16[8,256,256]{2,1,0:T(8,128)(2,1)}, bf16[32,160,1024]{2,1,0:T(8,128)(2,1)}) custom-call(bf16[2,128,2560]{2,1,0:T(8,128)(2,1)} %bitcast.40, bf16[2,128,2560]{2,1,0:T(8,128)(2,1)} %bitcast.41, bf16[160,1024]{1,0:T(8,128)(2,1)} %w_in.1, bf16[256,5120]{1,0:T(8,128)(2,1)} %bitcast.35), custom_call_target="tpu_custom_call" | custom-call | tf_op jit(solution)/shard_map/gather/pallas_call | solution.py:246
  103.8 30.8 %attention.1 = (bf16[16,64,640]{2,1,0:T(8,128)(2,1)}, f32[2,8,128,128]{3,2,1,0:T(8,128)}) custom-call(s32[9]{0:T(128)} %pad_add_fusion.act, bf16[16,64,640]{2,1,0:T(8,128)(2,1)} %bitcast.42, bf16[16,64,640]{2,1,0:T(8,128)(2,1)} %bitcast.43, bf16[16,128,256]{2,1,0:T(8,128)(2,1)} %bitcast.44), custom_call_target="tpu_custom_call" | custom-call | tf_op jit(solution)/shard_map/attention/pallas_call | solution.py:77
  134.6 80.5 %weight_gradient.1 = (f32[160,128]{1,0:T(8,128)}, bf16[256,1024]{1,0:T(8,128)(2,1)}, bf16[2,128,2560]{2,1,0:T(8,128)(2,1)}) custom-call(s32[16]{0:T(128)} %broadcast_subtract_fusion.inv, bf16[4,640,512]{2,1,0:T(8,128)(2,1)} %pad_maximum_fusion.x_ref, f32[2,8,128,128]{3,2,1,0:T(8,128)} %get-tuple-element.21.dk_ref, bf16[8,2,64,640]{3,2,1,0:T(8,128)(2,1)} %bitcast.38), custom_call_target="tpu_custom_call" | custom-call | tf_op jit(solution)/shard_map/weight_gradient/pallas_call | solution.py:394
  215.1 0.0 copy-start.1
  215.1 8.6 %fusion = bf16[1,256,5120]{2,1,0:T(8,128)(2,1)} fusion(bf16[256,1024]{1,0:T(8,128)(2,1)} %get-tuple-element.24, bf16[5120,1024]{1,0:T(8,128)(2,1)} %bitcast.45), kind=kOutput, calls=%fused_computation.1 | convolution fusion | flops 2685665280 | bytes 13631488 | tf_op jit(solution)/shard_map/dot_general | solution.py:451
  223.7 0.0 copy-done.1
  223.7 0.0 copy-start.2
  223.7 1.1 copy.26
  224.8 0.0 copy-done.2
  224.8 0.6 copy.27
  (1 shorter events, 0.0 us)
Async XLA Ops:
  5.2 1.8 copy-start
  6.4 3.4 %collective-permute-start = (bf16[4,640,256]{2,1,0:T(8,128)(2,1)}, bf16[4,640,256]{2,1,0:T(8,128)(2,1)}, u32[]{:S(2)}, u32[]{:S(2)}) collective-permute-start(bf16[4,640,256]{2,1,0:T(8,128)(2,1)} %bitcast.9), channel_id=1, source_target_pairs={{0,8},{8,0},{16,24},{24,16},{32,40},{40,32},{48,56},{56,48},{64,72... | collective-permute-start | bytes 3932168 | tf_op jit(solution)/shard_map/ppermute | solution.py:438
  7.0 0.7 copy-start.3
  215.1 8.7 %copy-start.1 = (bf16[2,128,2560]{2,1,0:T(8,128)(2,1)S(1)}, bf16[2,128,2560]{2,1,0:T(8,128)(2,1)}, u32[]{:S(2)}) copy-start(bf16[2,128,2560]{2,1,0:T(8,128)(2,1)} %get-tuple-element.23) | copy-start | bytes 3932164
  223.7 1.1 copy-start.2
